TPU v7x, 256 devices: a whole 4x4x8 slice. The times are simulated.
256 devices in a mesh: tm: 16 (over z, core), trace: 16 (over y, x).
Axes of the slice: x: 4, y: 4, z: 8, core: 2. Of those that a mesh axis runs over, the one named last changes fastest.
Arguments:
- observed: bfloat16 [256, 8192], P('trace', 'tm'), may hold values from -32 to 32
- sampled: int32 [256, 8192], P('trace', 'tm'), may hold values 0 or 1
- probes: bfloat16 [256, 256, 128], P(None, 'trace'), may hold values from -0.0234375 to 0.0234375
Outputs:
- completed: float32 [256, 8192], P('trace', 'tm')
All inputs are finite; a program needn't handle non-finite values. No bound on the sum of `sampled` on one device may be relied on, other than what follows from the above.
Results may differ from a plain program's by a relative error of at most 0.0004.
Values may be sent and summed in bfloat16 or wider, within the bound.
No kernel may reach another device: no remote copies, remote signals or barrier semaphores. Data moves between devices by JAX's collectives and lax.ppermute only.
A program may use at most 64 MiB of HBM per device.

v0:
```python
import functools

import jax
import jax.numpy as jnp
from jax import lax
from jax.experimental import pallas as pl
from jax.experimental.pallas import tpu as pltpu
from jax.sharding import PartitionSpec as P

F32 = jnp.float32
BF16 = jnp.bfloat16
HI = lax.Precision.HIGHEST
LANES = 128
SUB = 8


def from_behind(block, axis, distance):
    devices = range(lax.axis_size(axis))
    route = [(i - distance, i) for i in devices if i - distance in devices]
    return lax.ppermute(block, axis, route)


def correlate(signal, kernel, numbers):
    return lax.conv_general_dilated(
        signal, kernel, (1,), "VALID", dimension_numbers=numbers, preferred_element_type=jnp.float32
    )


def exchanged(block, axis):
    return lax.all_to_all(block, axis, 0, 0, tiled=True)


def to_all(block, axis):
    copies = lax.axis_size(axis)
    return exchanged(jnp.broadcast_to(block[None], (copies,) + block.shape), axis)


def inverse_of(gram, ranks):
    lane = lax.broadcasted_iota(jnp.int32, (SUB, ranks), 1)
    row = lax.broadcasted_iota(jnp.int32, (SUB, ranks), 0)
    rows = [gram[SUB * i : SUB * i + SUB] for i in range(ranks // SUB)]
    for k in range(ranks // SUB):
        panel = rows[k]
        start = SUB * k
        for s in range(SUB):
            column = panel[:, start + s : start + s + 1]
            pivot = panel[s : s + 1, start + s : start + s + 1]
            scaled = jnp.where(lane[:1] == start + s, 1.0, panel[s : s + 1]) / pivot
            rest = jnp.where(lane == start + s, 0.0, panel) - column * scaled
            panel = jnp.where(row == s, scaled, rest)
        inside = (lane >= start) & (lane < start + SUB)
        for i in range(ranks // SUB):
            if i == k:
                continue
            acc = jnp.where(inside, 0.0, rows[i])
            for s in range(SUB):
                acc = acc - rows[i][:, start + s : start + s + 1] * panel[s : s + 1]
            rows[i] = acc
        rows[k] = panel
    return jnp.concatenate(rows, axis=0)

def kernel(taps, core_ref, own_ref, other_ref, trace_ref, out_ref, s_ref, hankel, sums, sem):
    core = core_ref[0]
    first = pltpu.make_async_copy(own_ref, s_ref.at[core], sem.at[0])
    second = pltpu.make_async_copy(other_ref, s_ref.at[1 - core], sem.at[1])
    first.start(); second.start()
    lane = lax.broadcasted_iota(jnp.int32, (LANES, LANES), 1)
    row = lax.broadcasted_iota(jnp.int32, (LANES, LANES), 0)
    later = lane >= row
    tiles = hankel.shape[0]
    def build(n, _):
        a = jnp.broadcast_to(trace_ref[pl.ds(n, 1), :], (LANES, LANES))
        b = jnp.broadcast_to(trace_ref[pl.ds(n + 1, 1), :], (LANES, LANES))
        t = pltpu.roll(jnp.where(lane + row >= LANES - 1, a, b), 1, 1, stride=1, stride_axis=0)
        hankel[n] = t.astype(BF16)
        return 0
    lax.fori_loop(0, tiles, build, 0)
    first.wait(); second.wait()
    cores, pbs, halves, zs, prow, width = s_ref.shape
    ranks = pbs * prow
    nt = (((1,), (1,)), ((), ()))
    sums[...] = jnp.zeros_like(sums)
    def chunk(z, c, th):
        return s_ref[c, :, th, z].reshape(ranks, width)
    def accumulate(z, _):
        total = None
        for c in range(cores):
            for th in range(halves):
                n = (z * cores + c) * (2 * halves) + 2 * th
                sc = chunk(z, c, th)
                t0, t1, t2 = hankel[n], hankel[n + 1], hankel[n + 2]
                lhs = jnp.concatenate([jnp.concatenate([t0, t1], 1), jnp.concatenate([t1, t2], 1), sc], 0)
                d = lax.dot_general(lhs, sc, nt, preferred_element_type=F32)
                total = d if total is None else total + d
        sums[...] += total
        return 0
    lax.fori_loop(0, zs, accumulate, 0)
    inverse = inverse_of(sums[taps:], ranks)
    weights = jnp.dot(sums[:taps], inverse, precision=HI, preferred_element_type=F32)
    high = weights.astype(BF16)
    low = (weights - high.astype(F32)).astype(BF16)
    pair = jnp.concatenate([high, low], 1)
    flip = jnp.where(lane + row == LANES - 1, 1.0, 0.0).astype(BF16)
    g = jnp.concatenate(
        [jnp.dot(flip, pair[i : i + LANES], preferred_element_type=F32).astype(BF16) for i in range(0, taps, LANES)], 0
    )
    def spread(z, carry):
        behind, rolled = carry
        for c in range(cores):
            for th in range(halves):
                n = (z * cores + c) * (2 * halves) + 2 * th
                sc = chunk(z, c, th)
                y = jnp.dot(g, jnp.concatenate([sc, sc], 0), preferred_element_type=F32)
                for h in range(2):
                    u = y[:LANES, LANES * h : LANES * h + LANES] + behind
                    behind = y[LANES:, LANES * h : LANES * h + LANES]
                    now = pltpu.roll(u, 0, 1, stride=1, stride_axis=0)
                    v = jnp.where(later, now, rolled)
                    rolled = now
                    out_ref[pl.ds(n + h, 1), :] = jnp.sum(v, axis=0, keepdims=True)
        return behind, rolled
    zero = jnp.zeros((LANES, LANES), F32)
    lax.fori_loop(0, zs, spread, (zero, zero))
    t = lax.broadcasted_iota(jnp.int32, out_ref.shape, 0) * LANES + lax.broadcasted_iota(jnp.int32, out_ref.shape, 1)
    out_ref[...] = out_ref[...] / jnp.minimum(t + 1, taps).astype(F32)

def estimate_of(core, own, other, trace, taps):
    groups, zs, prow, width = own.shape
    shape = (groups // 2, 2, zs, prow, width)
    samples = trace.shape[0]
    blocks = samples // LANES
    padded = jnp.pad(trace.astype(F32), (0, 8 * LANES)).reshape(blocks + 8, LANES)
    ranks = groups // 2 * prow
    return pl.pallas_call(
        functools.partial(kernel, taps),
        out_shape=jax.ShapeDtypeStruct((blocks, LANES), F32),
        in_specs=[pl.BlockSpec(memory_space=pltpu.SMEM), pl.BlockSpec(memory_space=pl.ANY), pl.BlockSpec(memory_space=pl.ANY),
                  pl.BlockSpec(memory_space=pltpu.VMEM)],
        out_specs=pl.BlockSpec(memory_space=pltpu.VMEM),
        scratch_shapes=[pltpu.VMEM((2,) + shape, BF16), pltpu.VMEM((blocks + 1, LANES, LANES), BF16),
                        pltpu.VMEM((taps + ranks, ranks), F32), pltpu.SemaphoreType.DMA((2,))],
        name="estimate",
    )(core, own.reshape(shape), other.reshape(shape), padded)


def on_device(observed, sampled, probes):
    taps, traces, ranks = probes.shape
    width = observed.shape[1]
    blocks = lax.axis_size("tm")
    groups = lax.axis_size("trace")
    core = lax.axis_index("tm") % 2
    data = jnp.where(sampled == 1, observed, jnp.zeros_like(observed))
    tail = from_behind(data[:, :taps], "tm", -1)
    extended = jnp.concatenate([data, tail], axis=1)[:, : width + taps - 1]
    partial = correlate(extended[None], probes, ("NCW", "WIO", "NCW"))[0].astype(jnp.bfloat16)
    rows, half = ranks * 2 // groups, width // 2
    parts = partial.reshape(groups // 2, rows, 2, half).transpose(0, 2, 1, 3).reshape(groups, rows, half)
    mine = exchanged(parts, "trace").astype(jnp.float32).sum(0).astype(jnp.bfloat16)
    outgoing = jnp.concatenate(
        [jnp.broadcast_to(mine[None], (blocks, rows, half)), data.reshape(traces, 2, half)], axis=1
    )
    incoming = exchanged(outgoing, "tm")
    trace = incoming[:, rows:].reshape(blocks * width)
    column = incoming[:, :rows].reshape(blocks // 2, 2, rows, half)
    own = to_all(lax.dynamic_index_in_dim(column, core, 1, keepdims=False), "trace").reshape(
        groups, blocks // 2, rows, half
    )
    other = lax.ppermute(own, "tm", [(i, i ^ 1) for i in range(blocks)])
    estimate = estimate_of(core[None].astype(jnp.int32), own, other, trace, taps)
    back = exchanged(estimate.reshape(blocks, width), "tm")
    return jnp.where(sampled == 1, observed.astype(jnp.float32), back)


def solution(mesh):
    in_specs = (P("trace", "tm"), P("trace", "tm"), P(None, "trace", None))
    out_specs = P("trace", "tm")
    return jax.shard_map(
        on_device, mesh=mesh, in_specs=in_specs, out_specs=out_specs, check_vma=False
    )
```

profile of v0, /device:TPU:1, one launch (start us, length us, event | category | flops | bytes accessed | tf_op | source)
XLA Modules:
  0.0 110.8 jit_solution(9566588019872860631)
XLA Ops:
  0.0 0.0 copy-start
  0.0 0.9 broadcast_select_fusion
  0.9 5.1 %collective-permute-start = (bf16[16,256]{1,0:T(8,128)(2,1)S(1)}, bf16[16,256]{1,0:T(8,128)(2,1)S(1)}, u32[]{:S(2)}, u32[]{:S(2)}) collective-permute-start(bf16[16,256]{1,0:T(8,128)(2,1)S(1)} %slice.16), channel_id=1, source_target_pairs={{16,0},{32,16},{48,32},{64,48},{80,64},{96,80},{112,96},{128,112},... | collective-permute-start | bytes 24584 | tf_op jit(solution)/shard_map/ppermute | solution.py:20
  6.0 1.1 %collective-permute-done = bf16[16,256]{1,0:T(8,128)(2,1)S(1)} collective-permute-done((bf16[16,256]{1,0:T(8,128)(2,1)S(1)}, bf16[16,256]{1,0:T(8,128)(2,1)S(1)}, u32[]{:S(2)}, u32[]{:S(2)}) %collective-permute-start) | collective-permute-done | bytes 8224 | tf_op jit(solution)/shard_map/ppermute | solution.py:20
  7.1 0.9 copy.13
  8.1 0.0 copy-done
  8.1 7.8 %convolution_convert_fusion = bf16[1,128,512]{1,0,2:T(2,128)(2,1)S(1)} fusion(bf16[1,16,767]{1,0,2:T(2,128)(2,1)S(1)} %copy.13, bf16[256,16,128]{2,1,0:T(8,128)(2,1)S(1)} %copy-done), kind=kOutput, calls=%fused_computation | convolution fusion | flops 536936448 | bytes 1204192 | tf_op jit(solution)/shard_map/conv_general_dilated | solution.py:24
  15.9 0.1 copy.14
  16.1 0.7 copy.15
  16.8 6.8 %all-to-all-start = ((bf16[16,16,256]{2,1,0:T(8,128)(2,1)}), bf16[16,16,256]{2,1,0:T(8,128)(2,1)S(1)}, u32[]{:S(2)}, u32[]{:S(2)}) async-start(bf16[16,16,256]{2,1,0:T(8,128)(2,1)} %bitcast.3), calls=%async_computation | async-start | bytes 262144 | tf_op jit(solution)/shard_map/all_to_all | solution.py:30
  23.6 6.8 %all-to-all-done = bf16[16,16,256]{2,1,0:T(8,128)(2,1)S(1)} async-done(((bf16[16,16,256]{2,1,0:T(8,128)(2,1)}), bf16[16,16,256]{2,1,0:T(8,128)(2,1)S(1)}, u32[]{:S(2)}, u32[]{:S(2)}) %all-to-all-start) | async-done | bytes 131104 | tf_op jit(solution)/shard_map/all_to_all | solution.py:30
  30.4 0.7 pad_maximum_fusion
  31.1 9.0 %all-to-all-start.1 = ((bf16[16,18,256]{2,1,0:T(8,128)(2,1)}), bf16[16,18,256]{2,1,0:T(8,128)(2,1)S(1)}, u32[]{:S(2)}, u32[]{:S(2)}) async-start(bf16[16,18,256]{2,1,0:T(8,128)(2,1)} %pad_maximum_fusion), calls=%async_computation.1 | async-start | bytes 393216 | tf_op jit(solution)/shard_map/all_to_all | solution.py:30
  40.1 10.2 %all-to-all-done.1 = bf16[16,18,256]{2,1,0:T(8,128)(2,1)S(1)} async-done(((bf16[16,18,256]{2,1,0:T(8,128)(2,1)}), bf16[16,18,256]{2,1,0:T(8,128)(2,1)S(1)}, u32[]{:S(2)}, u32[]{:S(2)}) %all-to-all-start.1) | async-done | bytes 147488 | tf_op jit(solution)/shard_map/all_to_all | solution.py:30
  50.3 0.1 broadcast_in_dim.28
  50.4 19.7 %all_to_all.27 = bf16[16,8,16,256]{3,2,1,0:T(8,128)(2,1)S(1)} all-to-all(bf16[16,8,16,256]{3,2,1,0:T(8,128)(2,1)S(1)} %broadcast_in_dim.28), channel_id=1, replica_groups=mesh['tm'=16,'trace'=16] {'trace'}, dimensions={0} | all-to-all | bytes 2097152 | tf_op jit(solution)/shard_map/all_to_all | solution.py:30
  70.1 1.2 %collective-permute-start.1 = (bf16[16,8,16,256]{3,2,1,0:T(8,128)(2,1)S(1)}, bf16[16,8,16,256]{3,2,1,0:T(8,128)(2,1)S(1)}, u32[]{:S(2)}, u32[]{:S(2)}) collective-permute-start(bf16[16,8,16,256]{3,2,1,0:T(8,128)(2,1)S(1)} %all_to_all.27), channel_id=1, source_target_pairs={{0,16},{16,0},{32,48},{48,32},{64,80},{80,64},{96,112},{112,96},{1... | collective-permute-start | bytes 3145736 | tf_op jit(solution)/shard_map/ppermute | solution.py:168
  71.4 0.6 bitcast_convert_fusion.trace_ref
  72.0 1.6 %collective-permute-done.1 = bf16[16,8,16,256]{3,2,1,0:T(8,128)(2,1)S(1)} collective-permute-done((bf16[16,8,16,256]{3,2,1,0:T(8,128)(2,1)S(1)}, bf16[16,8,16,256]{3,2,1,0:T(8,128)(2,1)S(1)}, u32[]{:S(2)}, u32[]{:S(2)}) %collective-permute-start.1) | collective-permute-done | bytes 1048608 | tf_op jit(solution)/shard_map/ppermute | solution.py:168
  73.6 1.0 copy-done.2
  74.7 24.3 %estimate.1 = f32[64,128]{1,0:T(8,128)} custom-call(s32[1]{0:T(128)} %bitcast.core_ref, bf16[8,2,8,16,256]{4,3,2,1,0:T(8,128)(2,1)} %bitcast.21, bf16[8,2,8,16,256]{4,3,2,1,0:T(8,128)(2,1)} %bitcast.22, f32[72,128]{1,0:T(8,128)} %bitcast_convert_fusion.trace_ref), custom_call_target="tpu_custom_call" | custom-call | tf_op jit(solution)/shard_map/estimate/pallas_call | solution.py:134
  99.0 0.0 copy-start.3
  99.0 11.1 %all_to_all.28 = f32[16,1,512]{2,1,0:T(1,128)S(1)} all-to-all(f32[16,1,512]{2,1,0:T(1,128)} %bitcast.25), channel_id=1, replica_groups=mesh['tm'=16,'trace'=16] {'tm'}, dimensions={0} | all-to-all | bytes 65536 | tf_op jit(solution)/shard_map/all_to_all | solution.py:30
  110.1 0.6 bitcast_select_fusion
  (14 shorter events, 0.1 us)
Async XLA Ops:
  0.0 8.1 %copy-start = (bf16[256,16,128]{2,1,0:T(8,128)(2,1)S(1)}, bf16[256,16,128]{2,1,0:T(8,128)(2,1)}, u32[]{:S(2)}) copy-start(bf16[256,16,128]{2,1,0:T(8,128)(2,1)} %param.5) | copy-start | bytes 3145732
  0.9 6.3 %collective-permute-start = (bf16[16,256]{1,0:T(8,128)(2,1)S(1)}, bf16[16,256]{1,0:T(8,128)(2,1)S(1)}, u32[]{:S(2)}, u32[]{:S(2)}) collective-permute-start(bf16[16,256]{1,0:T(8,128)(2,1)S(1)} %slice.16), channel_id=1, source_target_pairs={{16,0},{32,16},{48,32},{64,48},{80,64},{96,80},{112,96},{128,112},... | collective-permute-start | bytes 24584 | tf_op jit(solution)/shard_map/ppermute | solution.py:20
  16.8 13.6 %all-to-all-start = ((bf16[16,16,256]{2,1,0:T(8,128)(2,1)}), bf16[16,16,256]{2,1,0:T(8,128)(2,1)S(1)}, u32[]{:S(2)}, u32[]{:S(2)}) async-start(bf16[16,16,256]{2,1,0:T(8,128)(2,1)} %bitcast.3), calls=%async_computation | async-start | bytes 262144 | tf_op jit(solution)/shard_map/all_to_all | solution.py:30
  31.1 19.2 %all-to-all-start.1 = ((bf16[16,18,256]{2,1,0:T(8,128)(2,1)}), bf16[16,18,256]{2,1,0:T(8,128)(2,1)S(1)}, u32[]{:S(2)}, u32[]{:S(2)}) async-start(bf16[16,18,256]{2,1,0:T(8,128)(2,1)} %pad_maximum_fusion), calls=%async_computation.1 | async-start | bytes 393216 | tf_op jit(solution)/shard_map/all_to_all | solution.py:30
  70.1 3.5 %copy-start.1 = (bf16[16,8,16,256]{3,2,1,0:T(8,128)(2,1)}, bf16[16,8,16,256]{3,2,1,0:T(8,128)(2,1)S(1)}, u32[]{:S(2)}) copy-start(bf16[16,8,16,256]{3,2,1,0:T(8,128)(2,1)S(1)} %all_to_all.27) | copy-start | bytes 3145732
  70.1 3.5 %collective-permute-start.1 = (bf16[16,8,16,256]{3,2,1,0:T(8,128)(2,1)S(1)}, bf16[16,8,16,256]{3,2,1,0:T(8,128)(2,1)S(1)}, u32[]{:S(2)}, u32[]{:S(2)}) collective-permute-start(bf16[16,8,16,256]{3,2,1,0:T(8,128)(2,1)S(1)} %all_to_all.27), channel_id=1, source_target_pairs={{0,16},{16,0},{32,48},{48,32},{64,80},{80,64},{96,112},{112,96},{1... | collective-permute-start | bytes 3145736 | tf_op jit(solution)/shard_map/ppermute | solution.py:168
  73.6 1.0 copy-start.2
  99.0 11.2 %copy-start.3 = (bf16[16,512]{1,0:T(8,128)(2,1)S(1)}, bf16[16,512]{1,0:T(8,128)(2,1)}, u32[]{:S(2)}) copy-start(bf16[16,512]{1,0:T(8,128)(2,1)} %param.3) | copy-start | bytes 49156
where the time goes:
time: 111 us
  blocking collectives  30.8 us (28%)
  Pallas kernels  24.3 us (22%)
  starting transfers between devices  22 us (20%)
  waiting for transfers between devices  19.8 us (18%)
  matrix products  7.85 us (7%)
  local copies, waits for them, and re-layouts  2.96 us (3%)
  other arithmetic  2.83 us (3%)
    all_to_all x2, blocking collectives, exchanged(): return lax.all_to_all(block, axis, 0, 0, tiled=True)  30.8 us
    pallas_call x1, Pallas kernels, estimate_of(): pl.pallas_call(functools.partial(kernel, taps), out_shape=jax.ShapeDtypeS...  24.3 us
    all_to_all x2, waiting for transfers between devices, exchanged(): return lax.all_to_all(block, axis, 0, 0, tiled=True)  17 us
    all_to_all x2, starting transfers between devices, exchanged(): return lax.all_to_all(block, axis, 0, 0, tiled=True)  15.7 us
    conv_general_dilated x1, matrix products, correlate(): lax.conv_general_dilated(signal, kernel, (1,), 'VALID', dimension_numbers...  7.85 us
    ppermute x1, starting transfers between devices, from_behind(): return lax.ppermute(block, axis, route)  5.11 us
  transfers between devices with their start and end apart: 4, of which 4 were waited for; matrix products, arithmetic and copies ran while one was open for 1% of the time, Pallas kernels for 0%

commit v1 on v0

v1 whole, which is shorter than its diff:
```python
import functools

import jax
import jax.numpy as jnp
from jax import lax
from jax.experimental import pallas as pl
from jax.experimental.pallas import tpu as pltpu
from jax.sharding import PartitionSpec as P

F32 = jnp.float32
BF16 = jnp.bfloat16
HI = lax.Precision.HIGHEST
LANES = 128
SUB = 8
PANEL = 32
STRIPE = 16
LIMIT = 20 << 20


def from_behind(block, axis, distance):
    devices = range(lax.axis_size(axis))
    route = [(i - distance, i) for i in devices if i - distance in devices]
    return lax.ppermute(block, axis, route)


def exchanged(block, axis):
    return lax.all_to_all(block, axis, 0, 0, tiled=True)


def to_all(block, axis):
    copies = lax.axis_size(axis)
    return exchanged(jnp.broadcast_to(block[None], (copies,) + block.shape), axis)


def sketch_kernel(data_ref, tail_ref, probes_ref, out_ref, total):
    traces, width = data_ref.shape
    ranks = probes_ref.shape[1]
    span = STRIPE * traces
    upper = LANES * traces
    total[...] = jnp.zeros_like(total)
    contract = (((0,), (0,)), ((), ()))
    window = jnp.concatenate([data_ref[...], tail_ref[...]], 1).astype(F32)
    length = window.shape[1]

    def stripe(q, window):
        moved = [window if i == 0 else pltpu.roll(window, length - i, 1) for i in range(STRIPE)]
        moved = [x.astype(BF16) for x in moved]
        start = pl.multiple_of(q * span, span)
        for base, first in ((0, 0), (upper, LANES)):
            right = jnp.concatenate([x[:, first : first + width] for x in moved], 0)
            left = probes_ref[pl.ds(base + start, span), :]
            total[...] += lax.dot_general(left, right, contract, preferred_element_type=F32)
        return pltpu.roll(window, length - STRIPE, 1)

    lax.fori_loop(0, LANES // STRIPE, stripe, window)
    groups, tiles, rows, lanes = out_ref.shape
    for g in range(groups):
        for i in range(tiles):
            p, t = g // 2 * rows, (g % 2 * tiles + i) * lanes
            out_ref[g, i] = total[p : p + rows, t : t + lanes].astype(BF16)


def sketch_of(data, tail, probes, groups):
    taps, traces, ranks = probes.shape
    width = data.shape[1]
    return pl.pallas_call(
        sketch_kernel,
        out_shape=jax.ShapeDtypeStruct((groups, width // 2 // LANES, 2 * ranks // groups, LANES), BF16),
        in_specs=[pl.BlockSpec(memory_space=pltpu.VMEM)] * 3,
        out_specs=pl.BlockSpec(memory_space=pltpu.VMEM),
        scratch_shapes=[pltpu.VMEM((ranks, width), F32)],
        name="sketch",
    )(data, tail, probes.reshape(taps * traces, ranks))


def inverse_of(gram, ranks):
    lane = lax.broadcasted_iota(jnp.int32, (SUB, ranks), 1)
    row = lax.broadcasted_iota(jnp.int32, (SUB, ranks), 0)
    everywhere = lambda x: jnp.broadcast_to(x, (SUB, ranks))
    rows = [gram[i : i + SUB] for i in range(0, ranks, SUB)]
    steps = PANEL // SUB
    for top in range(0, ranks, PANEL):
        panel = rows[top // SUB : top // SUB + steps]
        for m in range(steps):
            start = top + SUB * m
            inside = (lane >= start) & (lane < start + SUB)
            columns = [[everywhere(part[:, start + s : start + s + 1]) for s in range(SUB)] for part in panel]
            pivots = columns[m]
            for s in range(SUB):
                picked = [everywhere(column[s : s + 1]) for column in pivots]
                scale = 1.0 / picked[s]
                chosen = row == s
                left = pivots[s]
                for t in range(SUB):
                    if t == s:
                        continue
                    scaled = picked[t] * scale
                    pivots[t] = jnp.where(chosen, scaled, pivots[t] - left * scaled)
                pivots[s] = jnp.where(chosen, scale, -left * scale)
            unit = jnp.where(inside, jnp.where(lane == start + row, 1.0, 0.0), panel[m])
            solved = sum(pivots[s] * everywhere(unit[s : s + 1]) for s in range(SUB))
            spread = [everywhere(solved[s : s + 1]) for s in range(SUB)]
            for r in range(steps):
                if r != m:
                    panel[r] = jnp.where(inside, 0.0, panel[r]) - sum(columns[r][s] * spread[s] for s in range(SUB))
            panel[m] = solved
        done = jnp.concatenate(panel, 0)
        whole = jnp.concatenate(rows, 0)
        wide = lax.broadcasted_iota(jnp.int32, (ranks, ranks), 1)
        within = (wide >= top) & (wide < top + PANEL)
        change = jnp.dot(whole[:, top : top + PANEL], done, precision=HI, preferred_element_type=F32)
        new = jnp.where(within, 0.0, whole) - change
        rows = [new[i : i + SUB] for i in range(0, ranks, SUB)]
        rows[top // SUB : top // SUB + steps] = panel
    return jnp.concatenate(rows, axis=0)


def block_of(ref, *index):
    picked = ref[index[:-2] + (slice(None),) + index[-2:]]
    blocks, tiles, rows, lanes = picked.shape
    return jnp.concatenate([picked[:, i].reshape(blocks * rows, lanes) for i in range(tiles)], 1)


def add_products(first, sketch_ref, hankel_ref, sums_ref, core, taps):
    pbs, halves, zs, tiles = sketch_ref.shape[:4]
    contract = (((1,), (1,)), ((), ()))
    per = halves * tiles

    def accumulate(z, _):
        total = None
        for th in range(halves):
            n = (z * 2 + core) * per + tiles * th
            sc = block_of(sketch_ref, th, z)
            t0, t1, t2 = hankel_ref[n], hankel_ref[n + 1], hankel_ref[n + 2]
            lhs = jnp.concatenate([jnp.concatenate([t0, t1], 1), jnp.concatenate([t1, t2], 1), sc], 0)
            part = lax.dot_general(lhs, sc, contract, preferred_element_type=F32)
            total = part if total is None else total + part
        sums_ref[...] += total
        return 0

    if first:
        sums_ref[...] = jnp.zeros_like(sums_ref)
    lax.fori_loop(0, zs, accumulate, 0, unroll=2)


def prepare_kernel(taps, core_ref, own_ref, trace_ref, hankel_ref, sums_ref):
    lane = lax.broadcasted_iota(jnp.int32, (LANES, LANES), 1)
    row = lax.broadcasted_iota(jnp.int32, (LANES, LANES), 0)
    here = lane + row >= LANES - 1

    def build(n, _):
        a = jnp.broadcast_to(trace_ref[pl.ds(n, 1), :], (LANES, LANES))
        b = jnp.broadcast_to(trace_ref[pl.ds(n + 1, 1), :], (LANES, LANES))
        hankel_ref[n] = pltpu.roll(jnp.where(here, a, b), 1, 1, stride=1, stride_axis=0).astype(BF16)
        return 0

    lax.fori_loop(0, hankel_ref.shape[0], build, 0, unroll=5)
    add_products(True, own_ref, hankel_ref, sums_ref, core_ref[0], taps)


def estimate_kernel(taps, core_ref, own_ref, other_ref, hankel_ref, given_ref, out_ref, s_ref, sums, sem):
    core = core_ref[0]
    first = pltpu.make_async_copy(own_ref, s_ref.at[core], sem.at[0])
    second = pltpu.make_async_copy(other_ref, s_ref.at[1 - core], sem.at[1])
    first.start()
    second.start()
    sums[...] = given_ref[...]
    add_products(False, other_ref, hankel_ref, sums, 1 - core, taps)
    cores, pbs, halves, zs, tiles, prow, lanes = s_ref.shape
    ranks = pbs * prow
    lane = lax.broadcasted_iota(jnp.int32, (LANES, LANES), 1)
    row = lax.broadcasted_iota(jnp.int32, (LANES, LANES), 0)
    later = lane >= row
    inverse = inverse_of(sums[taps:], ranks)
    weights = jnp.dot(sums[:taps], inverse, precision=HI, preferred_element_type=F32)
    high = weights.astype(BF16)
    low = (weights - high.astype(F32)).astype(BF16)
    pair = jnp.concatenate([high, low], 1)
    flip = jnp.where(lane + row == LANES - 1, 1.0, 0.0).astype(BF16)
    g = jnp.concatenate(
        [jnp.dot(flip, pair[i : i + LANES], preferred_element_type=F32).astype(BF16) for i in range(0, taps, LANES)], 0
    )
    first.wait()
    second.wait()

    def spread(z, carry):
        behind, rolled = carry
        for c in range(cores):
            for th in range(halves):
                n = (z * cores + c) * halves * tiles + tiles * th
                sc = block_of(s_ref, c, th, z)
                y = jnp.dot(g, jnp.concatenate([sc, sc], 0), preferred_element_type=F32)
                for h in range(tiles):
                    u = y[:LANES, LANES * h : LANES * h + LANES] + behind
                    behind = y[LANES:, LANES * h : LANES * h + LANES]
                    now = pltpu.roll(u, 0, 1, stride=1, stride_axis=0)
                    v = jnp.where(later, now, rolled)
                    rolled = now
                    out_ref[pl.ds(n + h, 1), :] = jnp.sum(v, axis=0, keepdims=True)
        return behind, rolled

    zero = jnp.zeros((LANES, LANES), F32)
    lax.fori_loop(0, zs, spread, (zero, zero))
    t = lax.broadcasted_iota(jnp.int32, out_ref.shape, 0) * LANES + lax.broadcasted_iota(jnp.int32, out_ref.shape, 1)
    out_ref[...] = out_ref[...] / jnp.minimum(t + 1, taps).astype(F32)


def estimate_of(core, own, other, trace, taps):
    groups, zs, tiles, prow, lanes = own.shape
    shape = (groups // 2, 2, zs, tiles, prow, lanes)
    blocks = trace.shape[0]
    padded = jnp.pad(trace.astype(F32), ((0, SUB), (0, 0)))
    ranks = groups // 2 * prow
    own, other = own.reshape(shape), other.reshape(shape)
    smem, vmem = pl.BlockSpec(memory_space=pltpu.SMEM), pl.BlockSpec(memory_space=pltpu.VMEM)
    flops = blocks * LANES * ranks * (taps + ranks)
    hankel, sums = pl.pallas_call(
        functools.partial(prepare_kernel, taps),
        out_shape=(
            jax.ShapeDtypeStruct((blocks + 1, LANES, LANES), BF16),
            jax.ShapeDtypeStruct((taps + ranks, ranks), F32),
        ),
        in_specs=[smem, vmem, vmem],
        out_specs=(vmem, vmem),
        compiler_params=pltpu.CompilerParams(vmem_limit_bytes=LIMIT),
        cost_estimate=pl.CostEstimate(flops=flops, bytes_accessed=4 << 20, transcendentals=0),
        name="prepare",
    )(core, own, padded)
    return pl.pallas_call(
        functools.partial(estimate_kernel, taps),
        out_shape=jax.ShapeDtypeStruct((blocks, LANES), F32),
        in_specs=[smem, vmem, vmem, vmem, vmem],
        out_specs=vmem,
        scratch_shapes=[
            pltpu.VMEM((2,) + shape, BF16),
            pltpu.VMEM((taps + ranks, ranks), F32),
            pltpu.SemaphoreType.DMA((2,)),
        ],
        compiler_params=pltpu.CompilerParams(vmem_limit_bytes=LIMIT),
        cost_estimate=pl.CostEstimate(flops=4 * flops, bytes_accessed=8 << 20, transcendentals=0),
        name="estimate",
    )(core, own, other, hankel, sums)


def on_device(observed, sampled, probes):
    taps, traces, ranks = probes.shape
    width = observed.shape[1]
    blocks = lax.axis_size("tm")
    groups = lax.axis_size("trace")
    rows, tiles = ranks * 2 // groups, width // 2 // LANES
    lines = width // LANES
    core = (lax.axis_index("tm") & 1).astype(jnp.int32)
    even = core == 0
    data = jnp.where(sampled == 1, observed, jnp.zeros_like(observed))
    tail = from_behind(data[:, :taps], "tm", -1)
    parts = sketch_of(data, tail, probes, groups).reshape(groups, tiles * rows, LANES)
    slots = jnp.pad(data.reshape(traces, lines, LANES), ((0, 0), (0, -lines % SUB), (0, 0)))
    parts, slots, core, even = lax.optimization_barrier((parts, slots, core, even))
    mine = exchanged(parts, "trace").astype(F32).sum(0).astype(BF16)
    outgoing = jnp.concatenate([jnp.broadcast_to(mine[None], (blocks,) + mine.shape), slots], axis=1)
    incoming = exchanged(outgoing, "tm")
    trace = incoming[:, tiles * rows : tiles * rows + lines].reshape(blocks * lines, LANES)
    column = incoming[:, : tiles * rows].reshape(blocks // 2, 2, tiles, rows, LANES)
    kept = jnp.where(even, column[:, 0], column[:, 1])
    own = to_all(kept, "trace").reshape(groups, blocks // 2, tiles, rows, LANES)
    other = lax.ppermute(own, "tm", [(i, i ^ 1) for i in range(blocks)])
    estimate = estimate_of(core[None], own, other, trace, taps)
    back = exchanged(estimate.reshape(blocks, width), "tm")
    return jnp.where(sampled == 1, observed.astype(F32), back)


def solution(mesh):
    in_specs = (P("trace", "tm"), P("trace", "tm"), P(None, "trace", None))
    out_specs = P("trace", "tm")
    return jax.shard_map(
        on_device, mesh=mesh, in_specs=in_specs, out_specs=out_specs, check_vma=False
    )
```

time: 111 us -> 89.8 us (0.81)
  blocking collectives: 30.8 us -> 61.4 us
  waiting for transfers between devices: 19.8 us -> 1.09 us
  starting transfers between devices: 22 us -> 6.31 us
  matrix products: 7.85 us -> 0 us
  Pallas kernels: 24.3 us -> 18.2 us
  local copies, waits for them, and re-layouts: 2.96 us -> 0.86 us
  other arithmetic: 2.83 us -> 1.47 us
    all_to_all x2 -> x4, blocking collectives: 30.8 us -> 61.4 us  [exchanged(): return lax.all_to_all(block, axis, 0, 0, tiled=True)]
    all_to_all x2 -> x0, waiting for transfers between devices: 17 us -> none  [exchanged(): return lax.all_to_all(block, axis, 0, 0, tiled=True)]
    all_to_all x2 -> x0, starting transfers between devices: 15.7 us -> none  [exchanged(): return lax.all_to_all(block, axis, 0, 0, tiled=True)]
    conv_general_dilated x1 -> x0, matrix products: 7.85 us -> none  [correlate(): lax.conv_general_dilated(signal, kernel, (1,), 'VALID', dimension_numbers...]
    pallas_call x1 -> x3, Pallas kernels: 24.3 us -> 18.2 us  [the longest x1 10.2 us: estimate_of(): pl.pallas_call(functools.partial(estimate_kernel, taps), out_shape=jax.Sh...]
    ppermute x1, waiting for transfers between devices: 1.63 us -> 0.01 us  [on_device(): other = lax.ppermute(own, 'tm', [(i, i ^ 1) for i in range(blocks)])]
  transfers between devices with their start and end apart: 4 -> 2, of which waited for: 4 -> 1; matrix products, arithmetic and copies ran while one was open for 1% -> 0% of each run, Pallas kernels for 0% -> 3%
where the time goes in v1:
time: 89.8 us; the launch traced here: 89.5 us
  blocking collectives  61.4 us (68%)
  Pallas kernels  18.2 us (20%)
  starting transfers between devices  6.31 us (7%)
  other arithmetic  1.47 us (2%)
  waiting for transfers between devices  1.09 us (1%)
    all_to_all x4, blocking collectives, exchanged(): return lax.all_to_all(block, axis, 0, 0, tiled=True)  61.4 us
    pallas_call x1, Pallas kernels, estimate_of(): pl.pallas_call(functools.partial(estimate_kernel, taps), out_shape=jax.Sh...  10.2 us
    ppermute x1, starting transfers between devices, from_behind(): return lax.ppermute(block, axis, route)  5.11 us
    pallas_call x1, Pallas kernels, sketch_of(): pl.pallas_call(sketch_kernel, out_shape=jax.ShapeDtypeStruct((groups, wid...  5.02 us
    pallas_call x1, Pallas kernels, estimate_of(): pl.pallas_call(functools.partial(prepare_kernel, taps), out_shape=(jax.Sh...  3.03 us
  transfers between devices with their start and end apart: 2, of which 1 were waited for; matrix products, arithmetic and copies ran while one was open for 0% of the time, Pallas kernels for 3%

profile of v1, /device:TPU:1, one launch (start us, length us, event | category | flops | bytes accessed | tf_op | source)
XLA Modules:
  0.0 89.5 jit_solution(5086143928751805383)
XLA Ops:
  0.0 0.8 broadcast_select_fusion
  0.8 0.0 copy-start
  0.8 5.1 %collective-permute-start = (bf16[16,256]{1,0:T(8,128)(2,1)S(1)}, bf16[16,256]{1,0:T(8,128)(2,1)S(1)}, u32[]{:S(2)}, u32[]{:S(2)}) collective-permute-start(bf16[16,256]{1,0:T(8,128)(2,1)S(1)} %slice.20), channel_id=1, source_target_pairs={{16,0},{32,16},{48,32},{64,48},{80,64},{96,80},{112,96},{128,112},... | collective-permute-start | bytes 24584 | tf_op jit(solution)/shard_map/ppermute | solution.py:23
  6.0 1.1 %collective-permute-done.tail_ref = bf16[16,256]{1,0:T(8,128)(2,1)S(1)} collective-permute-done((bf16[16,256]{1,0:T(8,128)(2,1)S(1)}, bf16[16,256]{1,0:T(8,128)(2,1)S(1)}, u32[]{:S(2)}, u32[]{:S(2)}) %collective-permute-start) | collective-permute-done | bytes 8224 | tf_op jit(solution)/shard_map/ppermute | solution.py:23
  7.1 0.0 copy-start.2
  7.1 0.0 copy-done
  7.1 0.6 copy-done.2
  7.7 5.0 %sketch.1 = bf16[16,2,16,128]{3,2,1,0:T(8,128)(2,1)} custom-call(bf16[16,512]{1,0:T(8,128)(2,1)} %copy-done, bf16[16,256]{1,0:T(8,128)(2,1)} %copy-done.2, bf16[4096,128]{1,0:T(8,128)(2,1)} %bitcast.26), custom_call_target="tpu_custom_call" | custom-call | tf_op jit(solution)/shard_map/sketch/pallas_call | solution.py:66
  12.7 13.6 %all_to_all.27 = bf16[16,32,128]{2,1,0:T(8,128)(2,1)S(1)} all-to-all(bf16[16,32,128]{2,1,0:T(8,128)(2,1)} %bitcast.27), channel_id=1, replica_groups=mesh['tm'=16,'trace'=16] {'trace'}, dimensions={0} | all-to-all | bytes 262144 | tf_op jit(solution)/shard_map/all_to_all | solution.py:27
  26.3 18.3 %all_to_all.28 = bf16[16,40,128]{2,1,0:T(8,128)(2,1)S(1)} all-to-all(bf16[16,40,128]{2,1,0:T(8,128)(2,1)S(1)} %pad_maximum_fusion), channel_id=1, replica_groups=mesh['tm'=16,'trace'=16] {'tm'}, dimensions={0} | all-to-all | bytes 327680 | tf_op jit(solution)/shard_map/all_to_all | solution.py:27
  44.7 0.2 broadcast_in_dim.21
  44.9 19.7 %all_to_all.29 = bf16[16,8,2,16,128]{4,3,2,1,0:T(8,128)(2,1)S(1)} all-to-all(bf16[16,8,2,16,128]{4,3,2,1,0:T(8,128)(2,1)S(1)} %broadcast_in_dim.21), channel_id=1, replica_groups=mesh['tm'=16,'trace'=16] {'trace'}, dimensions={0} | all-to-all | bytes 2097152 | tf_op jit(solution)/shard_map/all_to_all | solution.py:27
  64.6 1.2 %collective-permute-start.1 = (bf16[16,8,2,16,128]{4,3,2,1,0:T(8,128)(2,1)S(1)}, bf16[16,8,2,16,128]{4,3,2,1,0:T(8,128)(2,1)S(1)}, u32[]{:S(2)}, u32[]{:S(2)}) collective-permute-start(bf16[16,8,2,16,128]{4,3,2,1,0:T(8,128)(2,1)S(1)} %all_to_all.29), channel_id=1, source_target_pairs={{0,16},{16,0},{32,48},{48,32},{64,80},{80,64},{96,112},{112,96},{1... | collective-permute-start | bytes 3145736 | tf_op jit(solution)/shard_map/ppermute | solution.py:266
  65.8 3.0 %prepare.1 = (bf16[65,128,128]{2,1,0:T(8,128)(2,1)S(1)}, f32[384,128]{1,0:T(8,128)S(1)}) custom-call(s32[1]{0:T(128)} %bitcast.2.core_ref, bf16[8,2,8,2,16,128]{5,4,3,2,1,0:T(8,128)(2,1)S(1)} %bitcast.22, f32[72,128]{1,0:T(8,128)S(1)} %pad_convert_fusion.trace_ref), custom_call_target="tpu_custom_call" | custom-call | flops 402653184 | bytes 4194304 | tf_op jit(solution)/shard_map/prepare/pallas_call | solution.py:217
  68.8 0.0 collective-permute-done.1
  68.9 0.0 copy-start.1
  68.9 10.2 %estimate.1 = f32[64,128]{1,0:T(8,128)S(1)} custom-call(s32[1]{0:T(128)} %bitcast.2.core_ref, bf16[8,2,8,2,16,128]{5,4,3,2,1,0:T(8,128)(2,1)S(1)} %bitcast.23, bf16[8,2,8,2,16,128]{5,4,3,2,1,0:T(8,128)(2,1)S(1)} %bitcast.25, bf16[65,128,128]{2,1,0:T(8,128)(2,1)S(1)} %get-tuple-element.15.hankel_ref, f32[384,128]{1,0:T(8,128)S(1)} %get-tuple-element.16.given_ref), custom_call_target="tpu_custom_call" | custom-call | flops 1610612736 | bytes 8388608 | tf_op jit(solution)/shard_map/estimate/pallas_call | solution.py:229
  79.0 9.8 %all_to_all.30 = f32[16,1,512]{2,1,0:T(1,128)S(1)} all-to-all(f32[16,1,512]{2,1,0:T(1,128)S(1)} %bitcast.24), channel_id=1, replica_groups=mesh['tm'=16,'trace'=16] {'tm'}, dimensions={0} | all-to-all | bytes 65536 | tf_op jit(solution)/shard_map/all_to_all | solution.py:27
  88.8 0.0 copy-done.1
  88.8 0.6 bitcast_select_fusion
  (10 shorter events, 0.1 us)
Async XLA Ops:
  0.8 6.3 %copy-start = (bf16[16,512]{1,0:T(8,128)(2,1)}, bf16[16,512]{1,0:T(8,128)(2,1)S(1)}, u32[]{:S(2)}) copy-start(bf16[16,512]{1,0:T(8,128)(2,1)S(1)} %get-tuple-element.17.data_ref) | copy-start | bytes 49156
  0.8 6.3 %collective-permute-start = (bf16[16,256]{1,0:T(8,128)(2,1)S(1)}, bf16[16,256]{1,0:T(8,128)(2,1)S(1)}, u32[]{:S(2)}, u32[]{:S(2)}) collective-permute-start(bf16[16,256]{1,0:T(8,128)(2,1)S(1)} %slice.20), channel_id=1, source_target_pairs={{16,0},{32,16},{48,32},{64,48},{80,64},{96,80},{112,96},{128,112},... | collective-permute-start | bytes 24584 | tf_op jit(solution)/shard_map/ppermute | solution.py:23
  7.1 0.6 copy-start.2
  64.6 4.3 %collective-permute-start.1 = (bf16[16,8,2,16,128]{4,3,2,1,0:T(8,128)(2,1)S(1)}, bf16[16,8,2,16,128]{4,3,2,1,0:T(8,128)(2,1)S(1)}, u32[]{:S(2)}, u32[]{:S(2)}) collective-permute-start(bf16[16,8,2,16,128]{4,3,2,1,0:T(8,128)(2,1)S(1)} %all_to_all.29), channel_id=1, source_target_pairs={{0,16},{16,0},{32,48},{48,32},{64,80},{80,64},{96,112},{112,96},{1... | collective-permute-start | bytes 3145736 | tf_op jit(solution)/shard_map/ppermute | solution.py:266
  68.9 20.0 %copy-start.1 = (bf16[16,512]{1,0:T(8,128)(2,1)S(1)}, bf16[16,512]{1,0:T(8,128)(2,1)}, u32[]{:S(2)}) copy-start(bf16[16,512]{1,0:T(8,128)(2,1)} %param.3) | copy-start | bytes 49156

commit v2 on v1

v2 whole, which is shorter than its diff:
```python
import functools

import jax
import jax.numpy as jnp
from jax import lax
from jax.experimental import pallas as pl
from jax.experimental.pallas import tpu as pltpu
from jax.sharding import PartitionSpec as P

F32 = jnp.float32
BF16 = jnp.bfloat16
HI = lax.Precision.HIGHEST
LANES = 128
SUB = 8
PANEL = 32
LIMIT = 20 << 20
ROWS = 16


def from_behind(block, axis, distance):
    devices = range(lax.axis_size(axis))
    route = [(i - distance, i) for i in devices if i - distance in devices]
    return lax.ppermute(block, axis, route)


def exchanged(block, axis):
    return lax.all_to_all(block, axis, 0, 0, tiled=True)


def to_all(block, axis):
    copies = lax.axis_size(axis)
    return exchanged(jnp.broadcast_to(block[None], (copies,) + block.shape), axis)


def sketch_kernel(half, early_ref, late_ref, probes_ref, *refs):
    even, odd = refs[-2:]
    out_ref = refs[1 if half else 0]
    if not half:
        refs[1][...] = probes_ref[...]
    traces = early_ref.shape[0]
    span = LANES // traces
    step = 2 * LANES
    samples = jnp.concatenate([early_ref[...], late_ref[...]], 1).astype(F32)
    length = samples.shape[1]
    width = early_ref.shape[1]
    moved = [samples if i == 0 else pltpu.roll(samples, length - i, 1) for i in range(span)]
    stacked = jnp.concatenate(moved, 0)
    for i in range(0, length, LANES):
        even[i : i + LANES] = stacked[:, i : i + LANES].T.astype(BF16)
    shifted = pltpu.roll(stacked, length - span, 1)
    for i in range(0, length, LANES):
        odd[i : i + LANES] = shifted[:, i : i + LANES].T.astype(BF16)
    total = None
    for q in range(probes_ref.shape[0] // step):
        first = 2 * span * q
        left = jnp.concatenate([even[first : first + width], odd[first : first + width]], 1)
        part = jnp.dot(left, probes_ref[step * q : step * q + step], preferred_element_type=F32)
        total = part if total is None else total + part
    rows = out_ref.shape[-2]
    for i in range(width // LANES):
        block = total[LANES * i : LANES * i + LANES].T.astype(BF16)
        for p in range(out_ref.shape[0]):
            if half:
                out_ref[p, half, i] = block[rows * p : rows * p + rows]
            else:
                out_ref[p, i] = block[rows * p : rows * p + rows]
    if half:
        out_ref[:, 0] = refs[0][...]


def sketch_of(half, early, late, probes, *given):
    ranks = probes.shape[1]
    length = early.shape[1] + late.shape[1]
    shape = (given[0].shape[:1] + (2,) + given[0].shape[1:]) if given else (ranks // ROWS, early.shape[1] // LANES, ROWS, LANES)
    vmem = pl.BlockSpec(memory_space=pltpu.VMEM)
    return pl.pallas_call(
        functools.partial(sketch_kernel, half),
        out_shape=(jax.ShapeDtypeStruct(shape, BF16),) + (() if half else (jax.ShapeDtypeStruct(probes.shape, BF16),)),
        in_specs=[vmem] * (3 + len(given)),
        out_specs=(vmem,) if half else (vmem, vmem),
        scratch_shapes=[pltpu.VMEM((length, LANES), BF16), pltpu.VMEM((length, LANES), BF16)],
        compiler_params=pltpu.CompilerParams(vmem_limit_bytes=LIMIT),
        cost_estimate=pl.CostEstimate(
            flops=2 * early.shape[1] * probes.size, bytes_accessed=2 * probes.size, transcendentals=0
        ),
        name="sketch",
    )(early, late, probes, *given)


def added(terms):
    while len(terms) > 1:
        terms = [sum(terms[i : i + 2]) for i in range(0, len(terms), 2)]
    return terms[0]


def inverse_of(gram, ranks, beside):
    lane = lax.broadcasted_iota(jnp.int32, (SUB, ranks), 1)
    row = lax.broadcasted_iota(jnp.int32, (SUB, ranks), 0)
    everywhere = lambda x: jnp.broadcast_to(x, (SUB, ranks))
    rows = [gram[i : i + SUB] for i in range(0, ranks, SUB)]
    steps = PANEL // SUB
    for top in range(0, ranks, PANEL):
        panel = rows[top // SUB : top // SUB + steps]
        for m in range(steps):
            start = top + SUB * m
            inside = (lane >= start) & (lane < start + SUB)
            columns = [[everywhere(part[:, start + s : start + s + 1]) for s in range(SUB)] for part in panel]
            pivots = columns[m]
            for s in range(SUB):
                picked = [everywhere(column[s : s + 1]) for column in pivots]
                scale = 1.0 / picked[s]
                chosen = row == s
                left = pivots[s]
                for t in range(SUB):
                    if t == s:
                        continue
                    scaled = picked[t] * scale
                    pivots[t] = jnp.where(chosen, scaled, pivots[t] - left * scaled)
                pivots[s] = jnp.where(chosen, scale, -left * scale)
            unit = jnp.where(inside, jnp.where(lane == start + row, 1.0, 0.0), panel[m])
            solved = added([pivots[s] * everywhere(unit[s : s + 1]) for s in range(SUB)])
            spread = [everywhere(solved[s : s + 1]) for s in range(SUB)]
            for r in range(steps):
                if r != m:
                    panel[r] = jnp.where(inside, 0.0, panel[r]) - added(
                        [columns[r][s] * spread[s] for s in range(SUB)]
                    )
            panel[m] = solved
            beside(start // SUB)
        done = jnp.concatenate(panel, 0)
        whole = jnp.concatenate(rows, 0)
        wide = lax.broadcasted_iota(jnp.int32, (ranks, ranks), 1)
        within = (wide >= top) & (wide < top + PANEL)
        change = jnp.dot(whole[:, top : top + PANEL], done, precision=HI, preferred_element_type=F32)
        new = jnp.where(within, 0.0, whole) - change
        rows = [new[i : i + SUB] for i in range(0, ranks, SUB)]
        rows[top // SUB : top // SUB + steps] = panel
    return jnp.concatenate(rows, axis=0)


def joined(parts):
    return jnp.concatenate([part.reshape(part.shape[0] * part.shape[1], part.shape[2]) for part in parts], 1)


def own_tiles(sketch_ref, r):
    return joined([sketch_ref[:, th, r] for th in range(sketch_ref.shape[1])])


def hankel_tiles(hankel_ref, n, halves):
    top = jnp.concatenate([hankel_ref[n + 2 * th] for th in range(halves)], 1)
    return jnp.concatenate([top, jnp.concatenate([hankel_ref[n + 2 * th + 1] for th in range(halves)], 1)], 0)


def add_products(sketch_ref, hankel_ref, sums_ref, core):
    halves, blocks = sketch_ref.shape[1:3]
    contract = (((1,), (1,)), ((), ()))

    def accumulate(r, _):
        sc = own_tiles(sketch_ref, r)
        lhs = jnp.concatenate([hankel_tiles(hankel_ref, 2 * halves * r + core, halves), sc], 0)
        sums_ref[...] += lax.dot_general(lhs, sc, contract, preferred_element_type=F32)
        return 0

    sums_ref[...] = jnp.zeros_like(sums_ref)
    lax.fori_loop(0, blocks, accumulate, 0, unroll=4)


def prepare_kernel(taps, core_ref, own_ref, trace_ref, hankel_ref, sums_ref):
    lane = lax.broadcasted_iota(jnp.int32, (LANES, LANES), 1)
    row = lax.broadcasted_iota(jnp.int32, (LANES, LANES), 0)
    here = lane + row >= LANES - 1

    def build(n, _):
        a = jnp.broadcast_to(trace_ref[pl.ds(n, 1), :], (LANES, LANES))
        b = jnp.broadcast_to(trace_ref[pl.ds(n + 1, 1), :], (LANES, LANES))
        hankel_ref[n] = pltpu.roll(jnp.where(here, a, b), 1, 1, stride=1, stride_axis=0).astype(BF16)
        return 0

    lax.fori_loop(0, hankel_ref.shape[0], build, 0, unroll=5)
    add_products(own_ref, hankel_ref, sums_ref, core_ref[0])


def estimate_kernel(taps, core_ref, own_ref, other_ref, hankel_ref, given_ref, out_ref, s_ref, sums, sem):
    core = core_ref[0]
    first = pltpu.make_async_copy(own_ref, s_ref.at[core], sem.at[0])
    second = pltpu.make_async_copy(other_ref, s_ref.at[1 - core], sem.at[1])
    first.start()
    second.start()
    sums[...] = given_ref[...]
    tiles, pbs, halves, blocks, prow, lanes = s_ref.shape
    ranks = pbs * prow
    lane = lax.broadcasted_iota(jnp.int32, (LANES, LANES), 1)
    row = lax.broadcasted_iota(jnp.int32, (LANES, LANES), 0)
    later = lane >= row
    contract = (((1,), (1,)), ((), ()))
    grams = []
    for r in range(blocks):
        sc = own_tiles(other_ref, r)
        grams.append(lax.dot_general(sc, sc, contract, preferred_element_type=F32))
    gram = sums[taps:] + added(grams)

    def beside(r):
        lhs = hankel_tiles(hankel_ref, 2 * halves * r + 1 - core, halves)
        sums[:taps] += lax.dot_general(lhs, own_tiles(other_ref, r), contract, preferred_element_type=F32)

    inverse = inverse_of(gram, ranks, beside)
    weights = jnp.dot(sums[:taps], inverse, precision=HI, preferred_element_type=F32)
    high = weights.astype(BF16)
    low = (weights - high.astype(F32)).astype(BF16)
    pair = jnp.concatenate([high, low], 1)
    flip = jnp.where(lane + row == LANES - 1, 1.0, 0.0).astype(BF16)
    g = jnp.concatenate(
        [jnp.dot(flip, pair[i : i + LANES], preferred_element_type=F32).astype(BF16) for i in range(0, taps, LANES)], 0
    )
    first.wait()
    second.wait()

    def spread(r, carry):
        behind, rolled = carry
        for th in range(halves):
            n = (r * halves + th) * tiles
            sc = joined([s_ref[i, :, th, r] for i in range(tiles)])
            y = jnp.dot(g, jnp.concatenate([sc, sc], 0), preferred_element_type=F32)
            for h in range(tiles):
                u = y[:LANES, LANES * h : LANES * h + LANES] + behind
                behind = y[LANES:, LANES * h : LANES * h + LANES]
                now = pltpu.roll(u, 0, 1, stride=1, stride_axis=0)
                v = jnp.where(later, now, rolled)
                rolled = now
                out_ref[pl.ds(n + h, 1), :] = jnp.sum(v, axis=0, keepdims=True)
        return behind, rolled

    zero = jnp.zeros((LANES, LANES), F32)
    lax.fori_loop(0, blocks, spread, (zero, zero), unroll=2)
    t = lax.broadcasted_iota(jnp.int32, out_ref.shape, 0) * LANES + lax.broadcasted_iota(jnp.int32, out_ref.shape, 1)
    out_ref[...] = out_ref[...] / jnp.minimum(t + 1, taps).astype(F32)


def estimate_of(core, own, other, trace, taps):
    groups, _, prow, lanes = own.shape
    shape = (groups // 2, 2) + own.shape[1:]
    blocks = trace.shape[0]
    padded = jnp.pad(trace.astype(F32), ((0, SUB), (0, 0)))
    ranks = groups // 2 * prow
    own, other = own.reshape(shape), other.reshape(shape)
    smem, vmem = pl.BlockSpec(memory_space=pltpu.SMEM), pl.BlockSpec(memory_space=pltpu.VMEM)
    flops = blocks * LANES * ranks * (taps + ranks)
    hankel, sums = pl.pallas_call(
        functools.partial(prepare_kernel, taps),
        out_shape=(
            jax.ShapeDtypeStruct((blocks + 1, LANES, LANES), BF16),
            jax.ShapeDtypeStruct((taps + ranks, ranks), F32),
        ),
        in_specs=[smem, vmem, vmem],
        out_specs=(vmem, vmem),
        compiler_params=pltpu.CompilerParams(vmem_limit_bytes=LIMIT),
        cost_estimate=pl.CostEstimate(flops=flops, bytes_accessed=4 << 20, transcendentals=0),
        name="prepare",
    )(core, own, padded)
    return pl.pallas_call(
        functools.partial(estimate_kernel, taps),
        out_shape=jax.ShapeDtypeStruct((blocks, LANES), F32),
        in_specs=[smem, vmem, vmem, vmem, vmem],
        out_specs=vmem,
        scratch_shapes=[
            pltpu.VMEM((2,) + shape, BF16),
            pltpu.VMEM((taps + ranks, ranks), F32),
            pltpu.SemaphoreType.DMA((2,)),
        ],
        compiler_params=pltpu.CompilerParams(vmem_limit_bytes=LIMIT),
        cost_estimate=pl.CostEstimate(flops=4 * flops, bytes_accessed=8 << 20, transcendentals=0),
        name="estimate",
    )(core, own, other, hankel, sums)


def on_device(observed, sampled, probes):
    taps, traces, ranks = probes.shape
    width = observed.shape[1]
    blocks = lax.axis_size("tm")
    groups = lax.axis_size("trace")
    rows, tiles = ranks * 2 // groups, width // 2 // LANES
    lines = width // LANES
    core = (lax.axis_index("tm") & 1).astype(jnp.int32)
    data = jnp.where(sampled == 1, observed, jnp.zeros_like(observed))
    middle = width // 2
    tail = from_behind(data[:, :middle], "tm", -1)
    slots = jnp.pad(data.reshape(traces, lines, LANES), ((0, 0), (0, -lines % SUB), (0, 0)))
    flat = probes.reshape(taps * traces, ranks)
    early, late = data[:, :middle], data[:, middle:]
    parts, flat = sketch_of(0, early, late, flat)
    (parts,) = sketch_of(1, late, tail, flat, parts)
    parts = parts.reshape(groups, tiles * rows, LANES)
    parts, slots, core = lax.optimization_barrier((parts, slots, core))
    mine = exchanged(parts, "trace").astype(F32).sum(0).astype(BF16).reshape(tiles, rows, LANES)
    lots = jnp.broadcast_to(mine[None], (blocks // tiles,) + mine.shape).reshape(blocks, rows, LANES)
    incoming = exchanged(jnp.concatenate([lots, slots], axis=1), "tm")
    trace = incoming[:, rows : rows + lines].reshape(blocks * lines, LANES)
    own = to_all(incoming[:, :rows], "trace").reshape(groups, blocks, rows, LANES)
    other = lax.ppermute(own, "tm", [(i, i ^ 1) for i in range(blocks)])
    estimate = estimate_of(core[None], own, other, trace, taps)
    back = exchanged(estimate.reshape(blocks, width), "tm")
    return jnp.where(sampled == 1, observed.astype(F32), back)


def solution(mesh):
    in_specs = (P("trace", "tm"), P("trace", "tm"), P(None, "trace", None))
    out_specs = P("trace", "tm")
    return jax.shard_map(
        on_device, mesh=mesh, in_specs=in_specs, out_specs=out_specs, check_vma=False
    )
```

time: 89.8 us -> 83.4 us (0.929)
  Pallas kernels: 18.2 us -> 14.1 us
  blocking collectives: 61.4 us -> 59.4 us
  waiting for transfers between devices: 1.09 us -> 0.01 us
    pallas_call x1 -> x2, Pallas kernels: 5.02 us -> 1.97 us  [sketch_of(): pl.pallas_call(functools.partial(sketch_kernel, half), out_shape=(jax.Sha...]
    all_to_all x4, blocking collectives: 61.4 us -> 59.4 us  [exchanged(): return lax.all_to_all(block, axis, 0, 0, tiled=True)]
    ppermute x1, waiting for transfers between devices: 1.09 us -> 0.01 us  [from_behind(): return lax.ppermute(block, axis, route)]
    pallas_call x1, Pallas kernels: 10.2 us -> 9.13 us  [estimate_of(): pl.pallas_call(functools.partial(estimate_kernel, taps), out_shape=jax.Sh...]
  transfers between devices with their start and end apart: 2 -> 2, of which waited for: 1 -> 0; matrix products, arithmetic and copies ran while one was open for 0% -> 0% of each run, Pallas kernels for 3% -> 5%
where the time goes in v2:
time: 83.4 us; the launch traced here: 83 us
  blocking collectives  59.4 us (71%)
  Pallas kernels  14.1 us (17%)
  starting transfers between devices  6.5 us (8%)
  local copies, waits for them, and re-layouts  1.47 us (2%)
  other arithmetic  1.45 us (2%)
    all_to_all x4, blocking collectives, exchanged(): return lax.all_to_all(block, axis, 0, 0, tiled=True)  59.4 us
    pallas_call x1, Pallas kernels, estimate_of(): pl.pallas_call(functools.partial(estimate_kernel, taps), out_shape=jax.Sh...  9.13 us
    ppermute x1, starting transfers between devices, from_behind(): return lax.ppermute(block, axis, route)  5.11 us
    pallas_call x1, Pallas kernels, estimate_of(): pl.pallas_call(functools.partial(prepare_kernel, taps), out_shape=(jax.Sh...  3.02 us
    pallas_call x2, Pallas kernels, sketch_of(): pl.pallas_call(functools.partial(sketch_kernel, half), out_shape=(jax.Sha...  1.97 us
  transfers between devices with their start and end apart: 2, of which 0 were waited for; matrix products, arithmetic and copies ran while one was open for 0% of the time, Pallas kernels for 5%

profile of v2, /device:TPU:1, one launch (start us, length us, event | category | flops | bytes accessed | tf_op | source)
XLA Modules:
  0.0 83.0 jit_solution(8256038668844281558)
XLA Ops:
  0.0 0.8 broadcast_select_fusion
  0.8 5.1 %collective-permute-start = (bf16[16,256]{1,0:T(8,128)(2,1)S(1)}, bf16[16,256]{1,0:T(8,128)(2,1)S(1)}, u32[]{:S(2)}, u32[]{:S(2)}) collective-permute-start(bf16[16,256]{1,0:T(8,128)(2,1)S(1)} %get-tuple-element.21.early_ref), channel_id=1, source_target_pairs={{16,0},{32,16},{48,32},{64,48},{80,64},{96,80},{112,96},{128,112},... | collective-permute-start | bytes 24584 | tf_op jit(solution)/shard_map/ppermute | solution.py:23
  5.9 0.0 copy-start
  5.9 1.2 %copy-done = bf16[256,16,128]{2,1,0:T(8,128)(2,1)S(1)} copy-done((bf16[256,16,128]{2,1,0:T(8,128)(2,1)S(1)}, bf16[256,16,128]{2,1,0:T(8,128)(2,1)}, u32[]{:S(2)}) %copy-start) | copy-done | bytes 1048600
  7.1 1.0 %sketch.2 = (bf16[8,2,16,128]{3,2,1,0:T(8,128)(2,1)S(1)}, bf16[4096,128]{1,0:T(8,128)(2,1)S(1)}) custom-call(bf16[16,256]{1,0:T(8,128)(2,1)S(1)} %get-tuple-element.21.early_ref, bf16[16,256]{1,0:T(8,128)(2,1)S(1)} %get-tuple-element.22.late_ref.early_ref, bf16[4096,128]{1,0:T(8,128)(2,1)S(1)} %bitcast.11), custom_call_target="tpu_custom_call" | custom-call | flops 268435456 | bytes 1048576 | tf_op jit(solution)/shard_map/sketch/pallas_call | solution.py:76
  8.2 0.0 collective-permute-done.late_ref
  8.2 1.0 %sketch.3 = bf16[8,2,2,16,128]{4,3,2,1,0:T(8,128)(2,1)S(1)} custom-call(bf16[16,256]{1,0:T(8,128)(2,1)S(1)} %get-tuple-element.22.late_ref.early_ref, bf16[16,256]{1,0:T(8,128)(2,1)S(1)} %collective-permute-done.late_ref, bf16[4096,128]{1,0:T(8,128)(2,1)S(1)} %get-tuple-element.12.probes_ref, bf16[8,2,16,128]{3,2,1,0:T(8,128)(2,1)S(1)} %get-tuple-element.13.refs_0_), custom_call_target="tpu_custom_call" | custom-call | flops 268435456 | bytes 1048576 | tf_op jit(solution)/shard_map/sketch/pallas_call | solution.py:76
  9.2 12.5 %all_to_all.27 = bf16[16,32,128]{2,1,0:T(8,128)(2,1)S(1)} all-to-all(bf16[16,32,128]{2,1,0:T(8,128)(2,1)S(1)} %bitcast.14), channel_id=1, replica_groups=mesh['tm'=16,'trace'=16] {'trace'}, dimensions={0} | all-to-all | bytes 262144 | tf_op jit(solution)/shard_map/all_to_all | solution.py:27
  21.8 17.4 %all_to_all.28 = bf16[16,24,128]{2,1,0:T(8,128)(2,1)S(1)} all-to-all(bf16[16,24,128]{2,1,0:T(8,128)(2,1)S(1)} %pad_maximum_fusion), channel_id=1, replica_groups=mesh['tm'=16,'trace'=16] {'tm'}, dimensions={0} | all-to-all | bytes 196608 | tf_op jit(solution)/shard_map/all_to_all | solution.py:27
  39.2 0.2 broadcast_in_dim.23
  39.4 19.6 %all_to_all.29 = bf16[16,16,16,128]{3,2,1,0:T(8,128)(2,1)S(1)} all-to-all(bf16[16,16,16,128]{3,2,1,0:T(8,128)(2,1)S(1)} %broadcast_in_dim.23), channel_id=1, replica_groups=mesh['tm'=16,'trace'=16] {'trace'}, dimensions={0} | all-to-all | bytes 2097152 | tf_op jit(solution)/shard_map/all_to_all | solution.py:27
  58.9 1.4 %collective-permute-start.1 = (bf16[16,16,16,128]{3,2,1,0:T(8,128)(2,1)S(1)}, bf16[16,16,16,128]{3,2,1,0:T(8,128)(2,1)S(1)}, u32[]{:S(2)}, u32[]{:S(2)}) collective-permute-start(bf16[16,16,16,128]{3,2,1,0:T(8,128)(2,1)S(1)} %all_to_all.29), channel_id=1, source_target_pairs={{0,16},{16,0},{32,48},{48,32},{64,80},{80,64},{96,112},{112,96},{1... | collective-permute-start | bytes 3145736 | tf_op jit(solution)/shard_map/ppermute | solution.py:299
  60.3 3.0 %prepare.1 = (bf16[65,128,128]{2,1,0:T(8,128)(2,1)S(1)}, f32[384,128]{1,0:T(8,128)S(1)}) custom-call(s32[1]{0:T(128)} %bitcast.2.core_ref, bf16[8,2,16,16,128]{4,3,2,1,0:T(8,128)(2,1)S(1)} %bitcast.12, f32[72,128]{1,0:T(8,128)S(1)} %pad_convert_fusion.trace_ref), custom_call_target="tpu_custom_call" | custom-call | flops 402653184 | bytes 4194304 | tf_op jit(solution)/shard_map/prepare/pallas_call | solution.py:248
  63.4 0.0 collective-permute-done.1
  63.4 0.0 copy-start.1
  63.4 9.1 %estimate.1 = f32[64,128]{1,0:T(8,128)S(1)} custom-call(s32[1]{0:T(128)} %bitcast.2.core_ref, bf16[8,2,16,16,128]{4,3,2,1,0:T(8,128)(2,1)S(1)} %bitcast.13, bf16[8,2,16,16,128]{4,3,2,1,0:T(8,128)(2,1)S(1)} %bitcast.16, bf16[65,128,128]{2,1,0:T(8,128)(2,1)S(1)} %get-tuple-element.17.hankel_ref, f32[384,128]{1,0:T(8,128)S(1)} %get-tuple-element.18.given_ref), custom_call_target="tpu_custom_call" | custom-call | flops 1610612736 | bytes 8388608 | tf_op jit(solution)/shard_map/estimate/pallas_call | solution.py:260
  72.5 9.9 %all_to_all.30 = f32[16,1,512]{2,1,0:T(1,128)S(1)} all-to-all(f32[16,1,512]{2,1,0:T(1,128)S(1)} %bitcast.15), channel_id=1, replica_groups=mesh['tm'=16,'trace'=16] {'tm'}, dimensions={0} | all-to-all | bytes 65536 | tf_op jit(solution)/shard_map/all_to_all | solution.py:27
  82.4 0.0 copy-done.1
  82.4 0.6 bitcast_select_fusion
  (9 shorter events, 0.1 us)
Async XLA Ops:
  0.8 7.4 %collective-permute-start = (bf16[16,256]{1,0:T(8,128)(2,1)S(1)}, bf16[16,256]{1,0:T(8,128)(2,1)S(1)}, u32[]{:S(2)}, u32[]{:S(2)}) collective-permute-start(bf16[16,256]{1,0:T(8,128)(2,1)S(1)} %get-tuple-element.21.early_ref), channel_id=1, source_target_pairs={{16,0},{32,16},{48,32},{64,48},{80,64},{96,80},{112,96},{128,112},... | collective-permute-start | bytes 24584 | tf_op jit(solution)/shard_map/ppermute | solution.py:23
  5.9 1.2 %copy-start = (bf16[256,16,128]{2,1,0:T(8,128)(2,1)S(1)}, bf16[256,16,128]{2,1,0:T(8,128)(2,1)}, u32[]{:S(2)}) copy-start(bf16[256,16,128]{2,1,0:T(8,128)(2,1)} %param.5) | copy-start | bytes 3145732
  58.9 4.4 %collective-permute-start.1 = (bf16[16,16,16,128]{3,2,1,0:T(8,128)(2,1)S(1)}, bf16[16,16,16,128]{3,2,1,0:T(8,128)(2,1)S(1)}, u32[]{:S(2)}, u32[]{:S(2)}) collective-permute-start(bf16[16,16,16,128]{3,2,1,0:T(8,128)(2,1)S(1)} %all_to_all.29), channel_id=1, source_target_pairs={{0,16},{16,0},{32,48},{48,32},{64,80},{80,64},{96,112},{112,96},{1... | collective-permute-start | bytes 3145736 | tf_op jit(solution)/shard_map/ppermute | solution.py:299
  63.4 19.0 %copy-start.1 = (bf16[16,512]{1,0:T(8,128)(2,1)S(1)}, bf16[16,512]{1,0:T(8,128)(2,1)}, u32[]{:S(2)}) copy-start(bf16[16,512]{1,0:T(8,128)(2,1)} %param.3) | copy-start | bytes 49156

commit v3 on v2

--- a/solution.py
+++ b/solution.py
@@ -162,7 +162,7 @@
         return 0
 
     sums_ref[...] = jnp.zeros_like(sums_ref)
-    lax.fori_loop(0, blocks, accumulate, 0, unroll=4)
+    lax.fori_loop(0, blocks, accumulate, 0, unroll=8)
 
 
 def prepare_kernel(taps, core_ref, own_ref, trace_ref, hankel_ref, sums_ref):
@@ -176,7 +176,7 @@
         hankel_ref[n] = pltpu.roll(jnp.where(here, a, b), 1, 1, stride=1, stride_axis=0).astype(BF16)
         return 0
 
-    lax.fori_loop(0, hankel_ref.shape[0], build, 0, unroll=5)
+    lax.fori_loop(0, hankel_ref.shape[0], build, 0, unroll=13)
     add_products(own_ref, hankel_ref, sums_ref, core_ref[0])
 
 
@@ -193,11 +193,8 @@
     row = lax.broadcasted_iota(jnp.int32, (LANES, LANES), 0)
     later = lane >= row
     contract = (((1,), (1,)), ((), ()))
-    grams = []
-    for r in range(blocks):
-        sc = own_tiles(other_ref, r)
-        grams.append(lax.dot_general(sc, sc, contract, preferred_element_type=F32))
-    gram = sums[taps:] + added(grams)
+    whole = jnp.concatenate([own_tiles(other_ref, r) for r in range(blocks)], 1)
+    gram = sums[taps:] + lax.dot_general(whole, whole, contract, preferred_element_type=F32)
 
     def beside(r):
         lhs = hankel_tiles(hankel_ref, 2 * halves * r + 1 - core, halves)

time: 83.4 us -> 82.9 us (level)
  Pallas kernels: 14.1 us -> 13.2 us
    pallas_call x1, Pallas kernels: 3.02 us -> 2.08 us  [estimate_of(): pl.pallas_call(functools.partial(prepare_kernel, taps), out_shape=(jax.Sh...]
  transfers between devices with their start and end apart: 2 -> 2, of which waited for: 0 -> 1; matrix products, arithmetic and copies ran while one was open for 0% -> 0% of each run, Pallas kernels for 5% -> 4%
where the time goes in v3:
time: 82.9 us; the launch traced here: 82.6 us
  blocking collectives  59.7 us (72%)
  Pallas kernels  13.2 us (16%)
  starting transfers between devices  6.5 us (8%)
  local copies, waits for them, and re-layouts  1.47 us (2%)
  other arithmetic  1.45 us (2%)
    all_to_all x4, blocking collectives, exchanged(): return lax.all_to_all(block, axis, 0, 0, tiled=True)  59.7 us
    pallas_call x1, Pallas kernels, estimate_of(): pl.pallas_call(functools.partial(estimate_kernel, taps), out_shape=jax.Sh...  9.1 us
    ppermute x1, starting transfers between devices, from_behind(): return lax.ppermute(block, axis, route)  5.11 us
    pallas_call x1, Pallas kernels, estimate_of(): pl.pallas_call(functools.partial(prepare_kernel, taps), out_shape=(jax.Sh...  2.08 us
    pallas_call x2, Pallas kernels, sketch_of(): pl.pallas_call(functools.partial(sketch_kernel, half), out_shape=(jax.Sha...  1.97 us
  transfers between devices with their start and end apart: 2, of which 1 were waited for; matrix products, arithmetic and copies ran while one was open for 0% of the time, Pallas kernels for 4%

profile of v3, /device:TPU:1, one launch (start us, length us, event | category | flops | bytes accessed | tf_op | source)
XLA Modules:
  0.0 82.6 jit_solution(6298003581914020627)
XLA Ops:
  0.0 0.8 broadcast_select_fusion
  0.8 5.1 %collective-permute-start = (bf16[16,256]{1,0:T(8,128)(2,1)S(1)}, bf16[16,256]{1,0:T(8,128)(2,1)S(1)}, u32[]{:S(2)}, u32[]{:S(2)}) collective-permute-start(bf16[16,256]{1,0:T(8,128)(2,1)S(1)} %get-tuple-element.21.early_ref), channel_id=1, source_target_pairs={{16,0},{32,16},{48,32},{64,48},{80,64},{96,80},{112,96},{128,112},... | collective-permute-start | bytes 24584 | tf_op jit(solution)/shard_map/ppermute | solution.py:23
  5.9 0.0 copy-start
  5.9 1.2 %copy-done = bf16[256,16,128]{2,1,0:T(8,128)(2,1)S(1)} copy-done((bf16[256,16,128]{2,1,0:T(8,128)(2,1)S(1)}, bf16[256,16,128]{2,1,0:T(8,128)(2,1)}, u32[]{:S(2)}) %copy-start) | copy-done | bytes 1048600
  7.1 1.0 %sketch.2 = (bf16[8,2,16,128]{3,2,1,0:T(8,128)(2,1)S(1)}, bf16[4096,128]{1,0:T(8,128)(2,1)S(1)}) custom-call(bf16[16,256]{1,0:T(8,128)(2,1)S(1)} %get-tuple-element.21.early_ref, bf16[16,256]{1,0:T(8,128)(2,1)S(1)} %get-tuple-element.22.late_ref.early_ref, bf16[4096,128]{1,0:T(8,128)(2,1)S(1)} %bitcast.11), custom_call_target="tpu_custom_call" | custom-call | flops 268435456 | bytes 1048576 | tf_op jit(solution)/shard_map/sketch/pallas_call | solution.py:76
  8.2 0.0 collective-permute-done.late_ref
  8.2 1.0 %sketch.3 = bf16[8,2,2,16,128]{4,3,2,1,0:T(8,128)(2,1)S(1)} custom-call(bf16[16,256]{1,0:T(8,128)(2,1)S(1)} %get-tuple-element.22.late_ref.early_ref, bf16[16,256]{1,0:T(8,128)(2,1)S(1)} %collective-permute-done.late_ref, bf16[4096,128]{1,0:T(8,128)(2,1)S(1)} %get-tuple-element.12.probes_ref, bf16[8,2,16,128]{3,2,1,0:T(8,128)(2,1)S(1)} %get-tuple-element.13.refs_0_), custom_call_target="tpu_custom_call" | custom-call | flops 268435456 | bytes 1048576 | tf_op jit(solution)/shard_map/sketch/pallas_call | solution.py:76
  9.2 12.5 %all_to_all.27 = bf16[16,32,128]{2,1,0:T(8,128)(2,1)S(1)} all-to-all(bf16[16,32,128]{2,1,0:T(8,128)(2,1)S(1)} %bitcast.14), channel_id=1, replica_groups=mesh['tm'=16,'trace'=16] {'trace'}, dimensions={0} | all-to-all | bytes 262144 | tf_op jit(solution)/shard_map/all_to_all | solution.py:27
  21.8 17.4 %all_to_all.28 = bf16[16,24,128]{2,1,0:T(8,128)(2,1)S(1)} all-to-all(bf16[16,24,128]{2,1,0:T(8,128)(2,1)S(1)} %pad_maximum_fusion), channel_id=1, replica_groups=mesh['tm'=16,'trace'=16] {'tm'}, dimensions={0} | all-to-all | bytes 196608 | tf_op jit(solution)/shard_map/all_to_all | solution.py:27
  39.2 0.2 broadcast_in_dim.23
  39.4 19.6 %all_to_all.29 = bf16[16,16,16,128]{3,2,1,0:T(8,128)(2,1)S(1)} all-to-all(bf16[16,16,16,128]{3,2,1,0:T(8,128)(2,1)S(1)} %broadcast_in_dim.23), channel_id=1, replica_groups=mesh['tm'=16,'trace'=16] {'trace'}, dimensions={0} | all-to-all | bytes 2097152 | tf_op jit(solution)/shard_map/all_to_all | solution.py:27
  58.9 1.4 %collective-permute-start.1 = (bf16[16,16,16,128]{3,2,1,0:T(8,128)(2,1)S(1)}, bf16[16,16,16,128]{3,2,1,0:T(8,128)(2,1)S(1)}, u32[]{:S(2)}, u32[]{:S(2)}) collective-permute-start(bf16[16,16,16,128]{3,2,1,0:T(8,128)(2,1)S(1)} %all_to_all.29), channel_id=1, source_target_pairs={{0,16},{16,0},{32,48},{48,32},{64,80},{80,64},{96,112},{112,96},{1... | collective-permute-start | bytes 3145736 | tf_op jit(solution)/shard_map/ppermute | solution.py:296
  60.3 2.1 %prepare.1 = (bf16[65,128,128]{2,1,0:T(8,128)(2,1)S(1)}, f32[384,128]{1,0:T(8,128)S(1)}) custom-call(s32[1]{0:T(128)} %bitcast.2.core_ref, bf16[8,2,16,16,128]{4,3,2,1,0:T(8,128)(2,1)S(1)} %bitcast.12, f32[72,128]{1,0:T(8,128)S(1)} %pad_convert_fusion.trace_ref), custom_call_target="tpu_custom_call" | custom-call | flops 402653184 | bytes 4194304 | tf_op jit(solution)/shard_map/prepare/pallas_call | solution.py:245
  62.4 0.2 collective-permute-done.1
  62.6 0.0 copy-start.1
  62.6 9.1 %estimate.1 = f32[64,128]{1,0:T(8,128)S(1)} custom-call(s32[1]{0:T(128)} %bitcast.2.core_ref, bf16[8,2,16,16,128]{4,3,2,1,0:T(8,128)(2,1)S(1)} %bitcast.13, bf16[8,2,16,16,128]{4,3,2,1,0:T(8,128)(2,1)S(1)} %bitcast.16, bf16[65,128,128]{2,1,0:T(8,128)(2,1)S(1)} %get-tuple-element.17.hankel_ref, f32[384,128]{1,0:T(8,128)S(1)} %get-tuple-element.18.given_ref), custom_call_target="tpu_custom_call" | custom-call | flops 1610612736 | bytes 8388608 | tf_op jit(solution)/shard_map/estimate/pallas_call | solution.py:257
  71.7 10.2 %all_to_all.30 = f32[16,1,512]{2,1,0:T(1,128)S(1)} all-to-all(f32[16,1,512]{2,1,0:T(1,128)S(1)} %bitcast.15), channel_id=1, replica_groups=mesh['tm'=16,'trace'=16] {'tm'}, dimensions={0} | all-to-all | bytes 65536 | tf_op jit(solution)/shard_map/all_to_all | solution.py:27
  81.9 0.0 copy-done.1
  82.0 0.6 bitcast_select_fusion
  (9 shorter events, 0.1 us)
Async XLA Ops:
  0.8 7.4 %collective-permute-start = (bf16[16,256]{1,0:T(8,128)(2,1)S(1)}, bf16[16,256]{1,0:T(8,128)(2,1)S(1)}, u32[]{:S(2)}, u32[]{:S(2)}) collective-permute-start(bf16[16,256]{1,0:T(8,128)(2,1)S(1)} %get-tuple-element.21.early_ref), channel_id=1, source_target_pairs={{16,0},{32,16},{48,32},{64,48},{80,64},{96,80},{112,96},{128,112},... | collective-permute-start | bytes 24584 | tf_op jit(solution)/shard_map/ppermute | solution.py:23
  5.9 1.2 %copy-start = (bf16[256,16,128]{2,1,0:T(8,128)(2,1)S(1)}, bf16[256,16,128]{2,1,0:T(8,128)(2,1)}, u32[]{:S(2)}) copy-start(bf16[256,16,128]{2,1,0:T(8,128)(2,1)} %param.5) | copy-start | bytes 3145732
  58.9 3.7 %collective-permute-start.1 = (bf16[16,16,16,128]{3,2,1,0:T(8,128)(2,1)S(1)}, bf16[16,16,16,128]{3,2,1,0:T(8,128)(2,1)S(1)}, u32[]{:S(2)}, u32[]{:S(2)}) collective-permute-start(bf16[16,16,16,128]{3,2,1,0:T(8,128)(2,1)S(1)} %all_to_all.29), channel_id=1, source_target_pairs={{0,16},{16,0},{32,48},{48,32},{64,80},{80,64},{96,112},{112,96},{1... | collective-permute-start | bytes 3145736 | tf_op jit(solution)/shard_map/ppermute | solution.py:296
  62.6 19.4 %copy-start.1 = (bf16[16,512]{1,0:T(8,128)(2,1)S(1)}, bf16[16,512]{1,0:T(8,128)(2,1)}, u32[]{:S(2)}) copy-start(bf16[16,512]{1,0:T(8,128)(2,1)} %param.3) | copy-start | bytes 49156
